TPU v7x, 32 devices: a whole 2x2x4 slice. The times are simulated.
32 devices in a mesh: grp: 4 (over z), dev: 8 (over y, x, core).
Axes of the slice: x: 2, y: 2, z: 4, core: 2. Of those that a mesh axis runs over, the one named last changes fastest.
Arguments:
- positions: float32 [3, 128, 544], P(None, ('grp', 'dev')), may hold values from -2 to 20, as said below
- rest_shape: float32 [3, 544], replicated, may hold values from -3 to 3
- stiffness: float32 [544, 544], replicated, may hold values from -0.25 to 0.25
- up_map: float32 [544, 152], replicated, may hold values from -0.25 to 0.25
- down_map: float32 [152, 544], replicated, may hold values from -0.5 to 0.5
- m2m: float32 [152, 152], replicated, may hold values from -0.5 to 0.5
- box_template: float32 [3, 152], replicated, may hold values from -1 to 1
- near_target: int32 [32, 2], P(('grp', 'dev')), may hold values from 0 to 3
- near_owner: int32 [32, 2], P(('grp', 'dev')), may hold values from 0 to 7, as said below
- near_cell: int32 [32, 2], P(('grp', 'dev')), may hold values from 0 to 3, as said below
- near_count: int32 [32], P(('grp', 'dev')), may hold values from 1 to 2, as said below
Outputs:
- new_positions: float32 [3, 128, 544], P(None, ('grp', 'dev'))
- velocity: float32 [3, 128, 544], P(None, ('grp', 'dev'))
Inputs may be any that keep to these rules, and one draw needn't show every extreme that they name: `positions`: each cell's points lie within about 1.2 of the cell's center; devices of one group sit on a grid of spacing 2.5, groups are 6 apart. `near_owner`: device e's slots name devices of e's own group other than e itself; at most 2 used slots of one device name the same owner, and device 0 uses all 2 slots with exactly 2 on each owner it names. `near_cell`: the source cells named by one device's used slots are distinct. `near_count`: the used slots come first; device 0 uses all of them.
All inputs are finite; a program needn't handle non-finite values.
Results may differ from a plain program's by a relative error of at most 0.0003.
Values sent between devices are 32-bit elements; how exact they have to be, the bound alone decides.
No kernel may reach another device: no remote copies, remote signals or barrier semaphores. Data moves between devices by JAX's collectives and lax.ppermute only.
A program may use at most 64 MiB of HBM per device.

v0:
```python
import jax
import jax.numpy as jnp
from jax import lax
from jax.sharding import PartitionSpec as P

NEAR = 2
STEPS = 2
EPSILON_SQ = 0.25
VISCOSITY = 0.039788735772973836
TIME_STEP = 0.1
SKALAK_HARDEN = 2.0
CHECK_RADIUS = 1.0
DEVICE_RADIUS = 1.5
GROUP_RADIUS = 6.0


def stokes(targets, sources, forces):
    delta_x = targets[0][:, None] - sources[0][None, :]
    delta_y = targets[1][:, None] - sources[1][None, :]
    delta_z = targets[2][:, None] - sources[2][None, :]
    square = delta_x * delta_x + delta_y * delta_y + delta_z * delta_z
    inverse = 1.0 / ((square + EPSILON_SQ) * jnp.sqrt(square + EPSILON_SQ))
    direct = (square + 2.0 * EPSILON_SQ) * inverse
    projected = (
        delta_x * forces[0][None, :] + delta_y * forces[1][None, :] + delta_z * forces[2][None, :]
    ) * inverse
    result = jnp.einsum("ts,ks->kt", direct, forces, precision=lax.Precision.HIGHEST)
    extra = jnp.stack(
        [
            jnp.sum(delta_x * projected, axis=1),
            jnp.sum(delta_y * projected, axis=1),
            jnp.sum(delta_z * projected, axis=1),
        ]
    )
    return VISCOSITY * (result + extra)


def membrane(points, rest_shape, stiffness):
    centroid = jnp.mean(points, axis=2, keepdims=True)
    strain = points - centroid - rest_shape[:, None, :]
    linear = jnp.dot(
        strain.reshape(-1, strain.shape[2]), stiffness, precision=lax.Precision.HIGHEST
    ).reshape(strain.shape)
    stretch = jnp.sum(linear * linear, axis=0)
    return -linear * (1.0 + SKALAK_HARDEN * stretch / (1.0 + stretch))


def box_far(checks, equivalents, centers, radius, weights, box_template):
    sources = centers[:, :, None] + radius * box_template[None]
    forces = equivalents * weights.astype(equivalents.dtype)[:, None, None]
    source_count = equivalents.shape[0] * equivalents.shape[2]
    flat_sources = jnp.transpose(sources, (1, 0, 2)).reshape(3, source_count)
    flat_forces = jnp.transpose(forces, (1, 0, 2)).reshape(3, source_count)
    return stokes(checks, flat_sources, flat_forces)


def body(
    positions,
    rest_shape,
    stiffness,
    up_map,
    down_map,
    m2m,
    box_template,
    near_target,
    near_owner,
    near_cell,
    near_count,
):
    own_device = lax.axis_index("dev")
    own_group = lax.axis_index("grp")
    dev_count = lax.axis_size("dev")
    cell_count = positions.shape[1]
    slot_ids = jnp.arange(NEAR, dtype=jnp.int32)
    owners = near_owner[0]
    cell_ids = near_cell[0]
    targets = near_target[0]
    in_use = slot_ids < near_count[0]
    onehot = (
        (targets[:, None] == jnp.arange(cell_count, dtype=jnp.int32)[None, :]) & in_use[:, None]
    ).astype(jnp.float32)
    source_rows = owners * cell_count + cell_ids
    points = positions
    velocity = jnp.zeros_like(positions)
    for step_index in range(STEPS):
        forces = membrane(points, rest_shape, stiffness)
        stacked = jnp.concatenate([points, forces], axis=0)
        source_pool = lax.all_gather(stacked, "dev", axis=1, tiled=True)
        sources = jnp.take(source_pool, source_rows, axis=1)
        receivers = jnp.take(points, targets, axis=1)
        near_tiles = jax.vmap(stokes, in_axes=(1, 1, 1), out_axes=1)(
            receivers, sources[:3], sources[3:]
        )
        near_velocity = jnp.einsum(
            "ksp,sc->kcp", near_tiles, onehot, precision=lax.Precision.HIGHEST
        )
        equivalent = jnp.dot(jnp.sum(forces, axis=1), up_map, precision=lax.Precision.HIGHEST)
        center = jnp.mean(points, axis=(1, 2))
        checks = center[:, None] + CHECK_RADIUS * box_template
        box_forces = lax.all_gather(equivalent[None], "dev", axis=0, tiled=True)
        places = lax.all_gather(center[None], "dev", axis=0, tiled=True)
        indices = jnp.arange(box_forces.shape[0], dtype=jnp.int32)
        added = box_far(
            checks, box_forces, places, DEVICE_RADIUS, indices != own_device, box_template
        )
        equivalent_sum = jnp.sum(box_forces, axis=0)
        center_sum = jnp.sum(places, axis=0)
        group_eq = jnp.dot(equivalent_sum, m2m, precision=lax.Precision.HIGHEST)
        group_center = center_sum / dev_count
        outer_box_forces = lax.all_gather(group_eq[None], "grp", axis=0, tiled=True)
        outer_places = lax.all_gather(group_center[None], "grp", axis=0, tiled=True)
        outer_indices = jnp.arange(outer_box_forces.shape[0], dtype=jnp.int32)
        outer_far = box_far(
            checks,
            outer_box_forces,
            outer_places,
            GROUP_RADIUS,
            outer_indices != own_group,
            box_template,
        )
        far_checks = added + outer_far
        far_surface = jnp.dot(far_checks, down_map, precision=lax.Precision.HIGHEST)
        velocity = far_surface[:, None, :] + near_velocity
        points = points + TIME_STEP * velocity
    return (points, velocity)


def solution(mesh):
    return jax.shard_map(
        body,
        mesh=mesh,
        in_specs=(
            P(None, ("grp", "dev"), None),
            P(),
            P(),
            P(),
            P(),
            P(),
            P(),
            P(("grp", "dev"), None),
            P(("grp", "dev"), None),
            P(("grp", "dev"), None),
            P(("grp", "dev")),
        ),
        out_specs=(P(None, ("grp", "dev"), None), P(None, ("grp", "dev"), None)),
        check_vma=False,
    )
```

profile of v0, /device:TPU:0, one launch (start us, length us, event | category | flops | bytes accessed | tf_op | source)
XLA Modules:
  0.0 156.4 jit_solution(3233264386179120395)
XLA Ops:
  0.7 1.4 dynamic-slice
  2.7 0.9 fusion.199
  3.6 0.1 broadcast_multiply_fusion.5
  3.7 0.8 broadcast_multiply_fusion
  4.4 15.1 %all-reduce = f32[24]{0:T(128)S(1)} all-reduce(f32[24]{0:T(128)S(1)} %get-tuple-element.90), channel_id=3, replica_groups=mesh['grp'=4,'dev'=8] {'dev'}, use_global_device_ids=true, to_apply=%add | all-reduce | flops 24 | bytes 192
  20.1 1.6 %multiply_reduce_fusion.1 = (f32[4,544]{1,0:T(4,128)S(1)}, f32[3,4,544]{2,1,0:T(4,128)S(1)}) fusion(f32[544,544]{1,0:T(8,128)S(1)} %copy-done, f32[3,4,544]{2,1,0:T(4,128)} %param.15, f32[3,544]{1,0:T(4,128)} %param.16, f32[3,4]{1,0:T(4,128)S(1)} %broadcast_multiply_fusion.3), kind=kOutput, calls=%fused_computation.219 | convolution fusion | flops 42638720 | bytes 1251248 | tf_op jit(solution)/shard_map/dot_general | solution.py:41
  21.8 0.5 convolution_bitcast_fusion.1
  22.3 8.1 %all-gather.8 = f32[8,3,152]{2,1,0:T(4,128)S(1)} all-gather(f32[1,3,152]{2,1,0:T(4,128)S(1)} %convolution_bitcast_fusion.1), channel_id=2, replica_groups=mesh['grp'=4,'dev'=8] {'dev'}, dimensions={0}, use_global_device_ids=true | all-gather | bytes 16416 | tf_op jit(solution)/shard_map/all_gather | solution.py:100
  30.8 1.1 fusion.81
  31.9 0.1 reshape.201
  32.0 1.3 convolution_add_fusion.5
  33.4 0.6 dynamic-slice.1
  34.6 0.1 multiply_dynamic-update-slice_fusion.1
  34.7 11.9 %all-reduce.1 = f32[12]{0:T(128)S(1)} all-reduce(f32[12]{0:T(128)S(1)} %multiply_dynamic-update-slice_fusion.1), channel_id=5, replica_groups=mesh['grp'=4,'dev'=8] {'grp'}, use_global_device_ids=true, to_apply=%add.1 | all-reduce | flops 12 | bytes 96
  46.7 0.1 copy.44
  47.1 0.2 convolution_bitcast_fusion.3
  47.3 13.2 %all-gather.9 = f32[4,3,152]{2,1,0:T(4,128)S(1)} all-gather(f32[1,3,152]{2,1,0:T(4,128)S(1)} %convolution_bitcast_fusion.3), channel_id=4, replica_groups=mesh['grp'=4,'dev'=8] {'grp'}, dimensions={0}, use_global_device_ids=true | all-gather | bytes 9120 | tf_op jit(solution)/shard_map/all_gather | solution.py:110
  60.9 0.7 fusion.107
  61.7 0.1 reshape.202
  61.8 0.8 fusion.73
  62.6 0.3 fusion.213
  63.0 10.3 %all_gather.34 = f32[6,32,544]{2,0,1:T(8,128)S(1)} all-gather(f32[6,4,544]{2,0,1:T(8,128)S(1)} %copy.45), channel_id=1, replica_groups=mesh['grp'=4,'dev'=8] {'dev'}, dimensions={1}, use_global_device_ids=true | all-gather | bytes 470016 | tf_op jit(solution)/shard_map/all_gather | solution.py:88
  73.3 0.6 gather_fusion
  74.1 0.6 gather_fusion.1
  74.8 4.4 %fusion.7 = (f32[2,544]{1,0:T(2,128)S(1)}, f32[2,544]{1,0:T(2,128)S(1)}, f32[2,544]{1,0:T(2,128)S(1)}) fusion(f32[2,544]{1,0:T(2,128)S(1)} %get-tuple-element.103, f32[2,544]{1,0:T(2,128)S(1)} %get-tuple-element.69, f32[2,544]{1,0:T(2,128)S(1)} %get-tuple-element.98, f32[2,544]{1,0:T(2,128)S(1)} %get-tuple-element.101, f32[2,544]{1,0:T(2,128)S(1)} %get-tuple-element.70, ...), kind=kLoop, calls=%fused_computation.31 | loop fusion | flops 13609792 | bytes 52224 | tf_op jit(solution)/shard_map/vmap()/reduce_sum | solution.py:30
  79.2 4.6 %fusion.67 = f32[3,2,544]{2,0,1:T(4,128)S(1)} fusion(f32[2,544]{1,0:T(2,128)S(1)} %get-tuple-element.101, f32[2,544]{1,0:T(2,128)S(1)} %get-tuple-element.70, f32[2,544]{1,0:T(2,128)S(1)} %get-tuple-element.102, f32[2,544]{1,0:T(2,128)S(1)} %get-tuple-element.71, f32[2,544]{1,0:T(2,128)S(1)} %get-tuple-element.103, f32[2,544]{1,0:T(2,128)S(1)} %get-tuple-element.69, ...), kind=kOutput, calls=%fused_computation.99 | convolution fusion | flops 29014784 | bytes 79616 | tf_op jit(solution)/shard_map/vmap(ts,ks->kt)/dot_general | solution.py:27
  84.5 0.4 fusion.198
  84.9 0.9 multiply_reduce_fusion
  85.9 0.5 convolution_bitcast_fusion
  86.3 8.1 %all-gather.10 = f32[8,3,152]{2,1,0:T(4,128)S(1)} all-gather(f32[1,3,152]{2,1,0:T(4,128)S(1)} %convolution_bitcast_fusion), channel_id=6, replica_groups=mesh['grp'=4,'dev'=8] {'dev'}, dimensions={0}, use_global_device_ids=true | all-gather | bytes 16416 | tf_op jit(solution)/shard_map/all_gather | solution.py:100
  94.5 0.2 convolution_bitcast_fusion.2
  94.7 13.2 %all-gather.11 = f32[4,3,152]{2,1,0:T(4,128)S(1)} all-gather(f32[1,3,152]{2,1,0:T(4,128)S(1)} %convolution_bitcast_fusion.2), channel_id=8, replica_groups=mesh['grp'=4,'dev'=8] {'grp'}, dimensions={0}, use_global_device_ids=true | all-gather | bytes 9120 | tf_op jit(solution)/shard_map/all_gather | solution.py:110
  108.4 11.8 %all-reduce.2 = f32[24]{0:T(128)S(1)} all-reduce(f32[24]{0:T(128)S(1)} %get-tuple-element.88), channel_id=7, replica_groups=mesh['grp'=4,'dev'=8] {'dev'}, use_global_device_ids=true, to_apply=%add.2 | all-reduce | flops 24 | bytes 192
  120.3 0.1 multiply_dynamic-update-slice_fusion
  120.4 8.6 %all-reduce.3 = f32[12]{0:T(128)S(1)} all-reduce(f32[12]{0:T(128)S(1)} %multiply_dynamic-update-slice_fusion), channel_id=9, replica_groups=mesh['grp'=4,'dev'=8] {'grp'}, use_global_device_ids=true, to_apply=%add.3 | all-reduce | flops 12 | bytes 96
  129.0 0.1 copy.50
  129.5 0.7 fusion.118
  131.0 1.1 fusion.92
  132.1 0.1 reshape.203
  132.2 1.3 convolution_add_fusion.4
  133.6 0.8 fusion.71
  134.4 0.3 fusion.214
  134.8 10.1 %all_gather.39 = f32[6,32,544]{2,0,1:T(8,128)S(1)} all-gather(f32[6,4,544]{2,0,1:T(8,128)S(1)} %copy.51), channel_id=1, replica_groups=mesh['grp'=4,'dev'=8] {'dev'}, dimensions={1}, use_global_device_ids=true | all-gather | bytes 470016 | tf_op jit(solution)/shard_map/all_gather | solution.py:88
  145.0 0.5 gather_fusion.2
  145.7 0.6 gather_fusion.3
  146.4 4.4 %fusion.18 = (f32[2,544]{1,0:T(2,128)S(1)}, f32[2,544]{1,0:T(2,128)S(1)}, f32[2,544]{1,0:T(2,128)S(1)}) fusion(f32[2,544]{1,0:T(2,128)S(1)} %bitcast.162, f32[2,544]{1,0:T(2,128)S(1)} %bitcast.171, f32[2,544]{1,0:T(2,128)S(1)} %bitcast.164, f32[2,544]{1,0:T(2,128)S(1)} %bitcast.158, f32[2,544]{1,0:T(2,128)S(1)} %bitcast.167, f32[2,544]{1,0:T(2,128)S(1)} %bitcast.165, ...), kind=kLoop, calls=%fused_computation.42 | loop fusion | flops 13609792 | bytes 52224 | tf_op jit(solution)/shard_map/vmap()/reduce_sum | solution.py:30
  150.9 4.6 %fusion.61 = f32[3,2,544]{2,0,1:T(4,128)S(1)} fusion(f32[2,544]{1,0:T(2,128)S(1)} %bitcast.159, f32[2,544]{1,0:T(2,128)S(1)} %bitcast.168, f32[2,544]{1,0:T(2,128)S(1)} %bitcast.161, f32[2,544]{1,0:T(2,128)S(1)} %bitcast.170, f32[2,544]{1,0:T(2,128)S(1)} %bitcast.163, f32[2,544]{1,0:T(2,128)S(1)} %bitcast.172, f32[6,2,544]{2,0,1:T(8,128)S(1)} %select_bitcast_fusion, ...), kind=kOutput, calls=%fused_computation.97 | convolution fusion | flops 29014784 | bytes 79616 | tf_op jit(solution)/shard_map/vmap(ts,ks->kt)/dot_general | solution.py:27
  155.4 0.9 multiply_add_fusion
  (128 shorter events, 4.4 us)
Async XLA Ops:
  0.6 19.5 %copy-start = (f32[544,544]{1,0:T(8,128)S(1)}, f32[544,544]{1,0:T(8,128)}, u32[]{:S(2)}) copy-start(f32[544,544]{1,0:T(8,128)} %param.17) | copy-start | bytes 3551236
  0.6 21.1 %copy-start.1 = (f32[544,152]{0,1:T(8,128)S(1)}, f32[544,152]{0,1:T(8,128)}, u32[]{:S(2)}) copy-start(f32[544,152]{0,1:T(8,128)} %param.18) | copy-start | bytes 992260
  32.0 1.3 copy-start.10
  32.0 15.1 %copy-start.4 = (f32[152,152]{1,0:T(8,128)S(1)}, f32[152,152]{1,0:T(8,128)}, u32[]{:S(2)}) copy-start(f32[152,152]{1,0:T(8,128)} %param.20) | copy-start | bytes 277252
  60.9 1.7 %copy-start.2 = (f32[152,544]{1,0:T(8,128)S(1)}, f32[152,544]{1,0:T(8,128)}, u32[]{:S(2)}) copy-start(f32[152,544]{1,0:T(8,128)} %param.19) | copy-start | bytes 992260
  61.7 1.2 copy-start.3
  61.8 11.6 %copy-start.7 = (s32[1,2]{1,0:T(1,128)S(1)}, s32[1,2]{1,0:T(1,128)}, u32[]{:S(2)}) copy-start(s32[1,2]{1,0:T(1,128)} %param.24) | copy-start | bytes 28
  61.8 11.5 %copy-start.8 = (s32[1,2]{1,0:T(1,128)S(1)}, s32[1,2]{1,0:T(1,128)}, u32[]{:S(2)}) copy-start(s32[1,2]{1,0:T(1,128)} %param.23) | copy-start | bytes 28
  62.6 11.4 %copy-start.9 = (s32[1,2]{1,0:T(1,128)S(1)}, s32[1,2]{1,0:T(1,128)}, u32[]{:S(2)}) copy-start(s32[1,2]{1,0:T(1,128)} %param.22) | copy-start | bytes 28
  79.2 5.7 %copy-start.5 = (f32[3,544]{1,0:T(4,128)S(1)}, f32[3,544]{1,0:T(4,128)}, u32[]{:S(2)}) copy-start(f32[3,544]{1,0:T(4,128)} %param.16) | copy-start | bytes 19588
  83.8 45.6 %copy-start.6 = (f32[3,152]{1,0:T(4,128)S(1)}, f32[3,152]{1,0:T(4,128)}, u32[]{:S(2)}) copy-start(f32[3,152]{1,0:T(4,128)} %param.21) | copy-start | bytes 5476
where the time goes:
time: 157 us; the launch traced here: 156 us
  blocking collectives  111 us (71%)
  matrix products  19.1 us (12%)
  other arithmetic  15.7 us (10%)
  local copies, waits for them, and re-layouts  7.79 us (5%)
  between operations  3.27 us (2%)
    unnamed x4, blocking collectives  47.4 us
    all_gather x2, blocking collectives, body(): outer_box_forces = lax.all_gather(group_eq[None], 'grp', axis=0, tiled=True)  26.5 us
    all_gather x2, blocking collectives, body(): source_pool = lax.all_gather(stacked, 'dev', axis=1, tiled=True)  20.4 us
    all_gather x2, blocking collectives, body(): box_forces = lax.all_gather(equivalent[None], 'dev', axis=0, tiled=True)  16.2 us
    dot_general x6, matrix products, stokes(): jnp.einsum('ts,ks->kt', direct, forces, precision=lax.Precision.HIGHEST)  13.4 us
    reduce_sum x6, other arithmetic, stokes(): jnp.sum(delta_x * projected, axis=1)  12.5 us

commit v1 on v0

--- a/solution.py
+++ b/solution.py
@@ -12,6 +12,19 @@
 CHECK_RADIUS = 1.0
 DEVICE_RADIUS = 1.5
 GROUP_RADIUS = 6.0
+
+
+def ring_gather(x, axis, dim):
+    count, here, width = (lax.axis_size(axis), lax.axis_index(axis), x.shape[dim])
+    ahead = [(i, (i + 1) % count) for i in range(count)]
+    out = jnp.zeros((*x.shape[:dim], count * width, *x.shape[dim + 1 :]), x.dtype)
+    carried = x
+    for turn in range(count):
+        owner = (here - turn) % count
+        out = lax.dynamic_update_slice_in_dim(out, carried, owner * width, axis=dim)
+        if turn < count - 1:
+            carried = lax.ppermute(carried, axis, ahead)
+    return out
 
 
 def stokes(targets, sources, forces):
@@ -107,7 +120,7 @@
         center_sum = jnp.sum(places, axis=0)
         group_eq = jnp.dot(equivalent_sum, m2m, precision=lax.Precision.HIGHEST)
         group_center = center_sum / dev_count
-        outer_box_forces = lax.all_gather(group_eq[None], "grp", axis=0, tiled=True)
+        outer_box_forces = ring_gather(group_eq[None], "grp", 0)
         outer_places = lax.all_gather(group_center[None], "grp", axis=0, tiled=True)
         outer_indices = jnp.arange(outer_box_forces.shape[0], dtype=jnp.int32)
         outer_far = box_far(

time: 157 us -> 156 us (level)
  blocking collectives: 111 us -> 87.8 us
  waiting for transfers between devices: 0 us -> 20.6 us
  starting transfers between devices: 0 us -> 1.67 us
    all_gather x2 -> x0, blocking collectives: 26.5 us -> none  [body(): outer_box_forces = lax.all_gather(group_eq[None], 'grp', axis=0, tiled=True)]
    ppermute x0 -> x6, waiting for transfers between devices: none -> 20.6 us  [ring_gather(): carried = lax.ppermute(carried, axis, ahead)]
    all_gather x2, blocking collectives: 16.2 us -> 18.7 us  [body(): box_forces = lax.all_gather(equivalent[None], 'dev', axis=0, tiled=True)]
    ppermute x0 -> x6, starting transfers between devices: none -> 1.67 us  [ring_gather(): carried = lax.ppermute(carried, axis, ahead)]
  transfers between devices with their start and end apart: 0 -> 6, of which waited for: 0 -> 4; matrix products, arithmetic and copies ran while one was open for 0% -> 20% of each run, Pallas kernels for 0% -> 0%
where the time goes in v1:
time: 156 us
  blocking collectives  87.8 us (56%)
  waiting for transfers between devices  20.6 us (13%)
  matrix products  19.1 us (12%)
  other arithmetic  15.4 us (10%)
  local copies, waits for them, and re-layouts  8.05 us (5%)
  between operations  3.4 us (2%)
  starting transfers between devices  1.67 us (1%)
    unnamed x4, blocking collectives  48.6 us
    ppermute x6, waiting for transfers between devices, ring_gather(): carried = lax.ppermute(carried, axis, ahead)  20.6 us
    all_gather x2, blocking collectives, body(): source_pool = lax.all_gather(stacked, 'dev', axis=1, tiled=True)  20.4 us
    all_gather x2, blocking collectives, body(): box_forces = lax.all_gather(equivalent[None], 'dev', axis=0, tiled=True)  18.7 us
    dot_general x6, matrix products, stokes(): jnp.einsum('ts,ks->kt', direct, forces, precision=lax.Precision.HIGHEST)  13.4 us
    reduce_sum x6, other arithmetic, stokes(): jnp.sum(delta_x * projected, axis=1)  12.5 us
  transfers between devices with their start and end apart: 6, of which 4 were waited for; matrix products, arithmetic and copies ran while one was open for 20% of the time, Pallas kernels for 0%

profile of v1, /device:TPU:0, one launch (start us, length us, event | category | flops | bytes accessed | tf_op | source)
XLA Modules:
  0.0 155.9 jit_solution(7812082428362876529)
XLA Ops:
  0.7 1.0 fusion.199
  1.7 0.5 copy-done
  2.2 1.6 %multiply_reduce_fusion.1 = (f32[4,544]{1,0:T(4,128)S(1)}, f32[3,4,544]{2,1,0:T(4,128)S(1)}) fusion(f32[544,544]{1,0:T(8,128)S(1)} %copy-done, f32[3,4,544]{2,1,0:T(4,128)} %param.15, f32[3,544]{1,0:T(4,128)} %param.16, f32[3,4]{1,0:T(4,128)S(1)} %broadcast_multiply_fusion.3), kind=kOutput, calls=%fused_computation.219 | convolution fusion | flops 42638720 | bytes 1251248 | tf_op jit(solution)/shard_map/dot_general | solution.py:54
  3.9 0.5 convolution_bitcast_fusion.1
  4.4 10.6 %all-gather.6 = f32[8,3,152]{2,1,0:T(4,128)S(1)} all-gather(f32[1,3,152]{2,1,0:T(4,128)S(1)} %convolution_bitcast_fusion.1), channel_id=2, replica_groups=mesh['grp'=4,'dev'=8] {'dev'}, dimensions={0}, use_global_device_ids=true | all-gather | bytes 16416 | tf_op jit(solution)/shard_map/all_gather | solution.py:113
  15.1 0.2 convolution_bitcast_fusion.3
  15.2 1.6 %collective-permute-start = (f32[1,3,152]{2,1,0:T(4,128)S(1)}, f32[1,3,152]{2,1,0:T(4,128)S(1)}, u32[]{:S(2)}, u32[]{:S(2)}) collective-permute-start(f32[1,3,152]{2,1,0:T(4,128)S(1)} %convolution_bitcast_fusion.3), channel_id=1, source_target_pairs={{0,8},{8,16},{16,24},{24,0},{1,9},{9,17},{17,25},{25,1},{2,10},{10... | collective-permute-start | bytes 5480 | tf_op jit(solution)/shard_map/ppermute | solution.py:26
  16.9 0.6 dynamic-slice
  18.1 0.1 broadcast_multiply_fusion.5
  18.2 12.9 %all-reduce = f32[24]{0:T(128)S(1)} all-reduce(f32[24]{0:T(128)S(1)} %get-tuple-element.90), channel_id=3, replica_groups=mesh['grp'=4,'dev'=8] {'dev'}, use_global_device_ids=true, to_apply=%add | all-reduce | flops 24 | bytes 192
  31.2 0.6 dynamic-slice.1
  32.6 0.1 multiply_dynamic-update-slice_fusion.1
  32.7 10.7 %all-reduce.1 = f32[12]{0:T(128)S(1)} all-reduce(f32[12]{0:T(128)S(1)} %multiply_dynamic-update-slice_fusion.1), channel_id=4, replica_groups=mesh['grp'=4,'dev'=8] {'grp'}, use_global_device_ids=true, to_apply=%add.1 | all-reduce | flops 12 | bytes 96
  44.5 10.3 %all_gather.27 = f32[6,32,544]{2,0,1:T(8,128)S(1)} all-gather(f32[6,4,544]{2,0,1:T(8,128)S(1)} %copy.60), channel_id=1, replica_groups=mesh['grp'=4,'dev'=8] {'dev'}, dimensions={1}, use_global_device_ids=true | all-gather | bytes 470016 | tf_op jit(solution)/shard_map/all_gather | solution.py:101
  54.9 0.6 gather_fusion
  55.5 0.6 gather_fusion.1
  56.3 4.4 %fusion.7 = (f32[2,544]{1,0:T(2,128)S(1)}, f32[2,544]{1,0:T(2,128)S(1)}, f32[2,544]{1,0:T(2,128)S(1)}) fusion(f32[2,544]{1,0:T(2,128)S(1)} %get-tuple-element.103, f32[2,544]{1,0:T(2,128)S(1)} %get-tuple-element.63, f32[2,544]{1,0:T(2,128)S(1)} %get-tuple-element.98, f32[2,544]{1,0:T(2,128)S(1)} %get-tuple-element.101, f32[2,544]{1,0:T(2,128)S(1)} %get-tuple-element.64, ...), kind=kLoop, calls=%fused_computation.31 | loop fusion | flops 13609792 | bytes 52224 | tf_op jit(solution)/shard_map/vmap()/reduce_sum | solution.py:43
  61.4 4.6 %fusion.67 = f32[3,2,544]{2,0,1:T(4,128)S(1)} fusion(f32[2,544]{1,0:T(2,128)S(1)} %get-tuple-element.101, f32[2,544]{1,0:T(2,128)S(1)} %get-tuple-element.64, f32[2,544]{1,0:T(2,128)S(1)} %get-tuple-element.102, f32[2,544]{1,0:T(2,128)S(1)} %get-tuple-element.65, f32[2,544]{1,0:T(2,128)S(1)} %get-tuple-element.103, f32[2,544]{1,0:T(2,128)S(1)} %get-tuple-element.63, ...), kind=kOutput, calls=%fused_computation.99 | convolution fusion | flops 29014784 | bytes 79616 | tf_op jit(solution)/shard_map/vmap(ts,ks->kt)/dot_general | solution.py:40
  65.9 1.1 fusion.81
  67.1 1.3 convolution_add_fusion.5
  68.5 5.3 %collective-permute-done.1 = f32[1,3,152]{2,1,0:T(4,128)S(1)} collective-permute-done((f32[1,3,152]{2,1,0:T(4,128)S(1)}, f32[1,3,152]{2,1,0:T(4,128)S(1)}, u32[]{:S(2)}, u32[]{:S(2)}) %collective-permute-start.1) | collective-permute-done | bytes 1856 | tf_op jit(solution)/shard_map/ppermute | solution.py:26
  74.3 4.9 %collective-permute-done.2 = f32[1,3,152]{2,1,0:T(4,128)S(1)} collective-permute-done((f32[1,3,152]{2,1,0:T(4,128)S(1)}, f32[1,3,152]{2,1,0:T(4,128)S(1)}, u32[]{:S(2)}, u32[]{:S(2)}) %collective-permute-start.2) | collective-permute-done | bytes 1856 | tf_op jit(solution)/shard_map/ppermute | solution.py:26
  79.3 0.3 dynamic_update_slice.27
  79.9 0.7 fusion.107
  80.7 0.8 fusion.73
  81.5 0.3 fusion.215
  81.8 0.4 fusion.198
  82.3 0.9 multiply_reduce_fusion
  83.2 0.5 convolution_bitcast_fusion
  83.7 8.1 %all-gather.7 = f32[8,3,152]{2,1,0:T(4,128)S(1)} all-gather(f32[1,3,152]{2,1,0:T(4,128)S(1)} %convolution_bitcast_fusion), channel_id=5, replica_groups=mesh['grp'=4,'dev'=8] {'dev'}, dimensions={0}, use_global_device_ids=true | all-gather | bytes 16416 | tf_op jit(solution)/shard_map/all_gather | solution.py:113
  92.0 0.2 convolution_bitcast_fusion.2
  92.2 0.1 broadcast_multiply_fusion.4
  92.3 13.2 %all-reduce.2 = f32[24]{0:T(128)S(1)} all-reduce(f32[24]{0:T(128)S(1)} %get-tuple-element.88), channel_id=6, replica_groups=mesh['grp'=4,'dev'=8] {'dev'}, use_global_device_ids=true, to_apply=%add.2 | all-reduce | flops 24 | bytes 192
  106.5 10.1 %all_gather.31 = f32[6,32,544]{2,0,1:T(8,128)S(1)} all-gather(f32[6,4,544]{2,0,1:T(8,128)S(1)} %copy.69), channel_id=1, replica_groups=mesh['grp'=4,'dev'=8] {'dev'}, dimensions={1}, use_global_device_ids=true | all-gather | bytes 470016 | tf_op jit(solution)/shard_map/all_gather | solution.py:101
  116.6 0.5 gather_fusion.2
  117.3 0.6 gather_fusion.3
  118.0 4.4 %fusion.18 = (f32[2,544]{1,0:T(2,128)S(1)}, f32[2,544]{1,0:T(2,128)S(1)}, f32[2,544]{1,0:T(2,128)S(1)}) fusion(f32[2,544]{1,0:T(2,128)S(1)} %bitcast.162, f32[2,544]{1,0:T(2,128)S(1)} %bitcast.171, f32[2,544]{1,0:T(2,128)S(1)} %bitcast.164, f32[2,544]{1,0:T(2,128)S(1)} %bitcast.158, f32[2,544]{1,0:T(2,128)S(1)} %bitcast.167, f32[2,544]{1,0:T(2,128)S(1)} %bitcast.165, ...), kind=kLoop, calls=%fused_computation.42 | loop fusion | flops 13609792 | bytes 52224 | tf_op jit(solution)/shard_map/vmap()/reduce_sum | solution.py:43
  122.5 0.3 multiply_dynamic-update-slice_fusion
  122.8 4.6 %fusion.61 = f32[3,2,544]{2,0,1:T(4,128)S(1)} fusion(f32[2,544]{1,0:T(2,128)S(1)} %bitcast.159, f32[2,544]{1,0:T(2,128)S(1)} %bitcast.168, f32[2,544]{1,0:T(2,128)S(1)} %bitcast.161, f32[2,544]{1,0:T(2,128)S(1)} %bitcast.170, f32[2,544]{1,0:T(2,128)S(1)} %bitcast.163, f32[2,544]{1,0:T(2,128)S(1)} %bitcast.172, f32[6,2,544]{2,0,1:T(8,128)S(1)} %select_bitcast_fusion, ...), kind=kOutput, calls=%fused_computation.97 | convolution fusion | flops 29014784 | bytes 79616 | tf_op jit(solution)/shard_map/vmap(ts,ks->kt)/dot_general | solution.py:40
  127.3 1.1 fusion.92
  128.5 1.3 convolution_add_fusion.4
  129.8 11.9 %all-reduce.3 = f32[12]{0:T(128)S(1)} all-reduce(f32[12]{0:T(128)S(1)} %multiply_dynamic-update-slice_fusion), channel_id=7, replica_groups=mesh['grp'=4,'dev'=8] {'grp'}, use_global_device_ids=true, to_apply=%add.3 | all-reduce | flops 12 | bytes 96
  141.9 5.3 %collective-permute-done.4 = f32[1,3,152]{2,1,0:T(4,128)S(1)} collective-permute-done((f32[1,3,152]{2,1,0:T(4,128)S(1)}, f32[1,3,152]{2,1,0:T(4,128)S(1)}, u32[]{:S(2)}, u32[]{:S(2)}) %collective-permute-start.4) | collective-permute-done | bytes 1856 | tf_op jit(solution)/shard_map/ppermute | solution.py:26
  147.7 4.9 %collective-permute-done.5 = f32[1,3,152]{2,1,0:T(4,128)S(1)} collective-permute-done((f32[1,3,152]{2,1,0:T(4,128)S(1)}, f32[1,3,152]{2,1,0:T(4,128)S(1)}, u32[]{:S(2)}, u32[]{:S(2)}) %collective-permute-start.5) | collective-permute-done | bytes 1856 | tf_op jit(solution)/shard_map/ppermute | solution.py:26
  153.1 0.7 fusion.118
  153.8 0.8 fusion.71
  154.7 0.3 fusion.216
  155.0 0.9 multiply_add_fusion
  (156 shorter events, 5.2 us)
Async XLA Ops:
  0.6 1.6 %copy-start = (f32[544,544]{1,0:T(8,128)S(1)}, f32[544,544]{1,0:T(8,128)}, u32[]{:S(2)}) copy-start(f32[544,544]{1,0:T(8,128)} %param.17) | copy-start | bytes 3551236
  0.6 16.2 %copy-start.11 = (u32[32]{0:T(128)S(1)}, u32[32]{0:T(128)}, u32[]{:S(2)}) copy-start(u32[32]{0:T(128)} %constant.118) | copy-start | bytes 388
  0.7 30.6 %copy-start.10 = (u32[32]{0:T(128)S(1)}, u32[32]{0:T(128)}, u32[]{:S(2)}) copy-start(u32[32]{0:T(128)} %constant.123) | copy-start | bytes 388
  0.7 3.2 %copy-start.1 = (f32[544,152]{0,1:T(8,128)S(1)}, f32[544,152]{0,1:T(8,128)}, u32[]{:S(2)}) copy-start(f32[544,152]{0,1:T(8,128)} %param.18) | copy-start | bytes 992260
  0.7 14.4 %copy-start.4 = (f32[152,152]{1,0:T(8,128)S(1)}, f32[152,152]{1,0:T(8,128)}, u32[]{:S(2)}) copy-start(f32[152,152]{1,0:T(8,128)} %param.20) | copy-start | bytes 277252
  0.7 16.2 %copy-start.9 = (s32[1,2]{1,0:T(1,128)S(1)}, s32[1,2]{1,0:T(1,128)}, u32[]{:S(2)}) copy-start(s32[1,2]{1,0:T(1,128)} %param.22) | copy-start | bytes 28
  0.7 42.8 %copy-start.6 = (f32[3,152]{1,0:T(4,128)S(1)}, f32[3,152]{1,0:T(4,128)}, u32[]{:S(2)}) copy-start(f32[3,152]{1,0:T(4,128)} %param.21) | copy-start | bytes 5476
  0.7 43.8 %copy-start.3 = (f32[3,4,544]{2,1,0:T(4,128)S(1)}, f32[3,4,544]{2,1,0:T(4,128)}, u32[]{:S(2)}) copy-start(f32[3,4,544]{2,1,0:T(4,128)} %param.15) | copy-start | bytes 78340
  3.8 51.0 %copy-start.7 = (s32[1,2]{1,0:T(1,128)S(1)}, s32[1,2]{1,0:T(1,128)}, u32[]{:S(2)}) copy-start(s32[1,2]{1,0:T(1,128)} %param.24) | copy-start | bytes 28
  3.8 51.0 %copy-start.8 = (s32[1,2]{1,0:T(1,128)S(1)}, s32[1,2]{1,0:T(1,128)}, u32[]{:S(2)}) copy-start(s32[1,2]{1,0:T(1,128)} %param.23) | copy-start | bytes 28
  15.2 53.1 %collective-permute-start = (f32[1,3,152]{2,1,0:T(4,128)S(1)}, f32[1,3,152]{2,1,0:T(4,128)S(1)}, u32[]{:S(2)}, u32[]{:S(2)}) collective-permute-start(f32[1,3,152]{2,1,0:T(4,128)S(1)} %convolution_bitcast_fusion.3), channel_id=1, source_target_pairs={{0,8},{8,16},{16,24},{24,0},{1,9},{9,17},{17,25},{25,1},{2,10},{10... | collective-permute-start | bytes 5480 | tf_op jit(solution)/shard_map/ppermute | solution.py:26
  68.4 5.5 %collective-permute-start.1 = (f32[1,3,152]{2,1,0:T(4,128)S(1)}, f32[1,3,152]{2,1,0:T(4,128)S(1)}, u32[]{:S(2)}, u32[]{:S(2)}) collective-permute-start(f32[1,3,152]{2,1,0:T(4,128)S(1)} %collective-permute-done), channel_id=1, source_target_pairs={{0,8},{8,16},{16,24},{24,0},{1,9},{9,17},{17,25},{25,1},{2,10},{10... | collective-permute-start | bytes 5480 | tf_op jit(solution)/shard_map/ppermute | solution.py:26
  73.8 5.4 %collective-permute-start.2 = (f32[1,3,152]{2,1,0:T(4,128)S(1)}, f32[1,3,152]{2,1,0:T(4,128)S(1)}, u32[]{:S(2)}, u32[]{:S(2)}) collective-permute-start(f32[1,3,152]{2,1,0:T(4,128)S(1)} %collective-permute-done.1), channel_id=1, source_target_pairs={{0,8},{8,16},{16,24},{24,0},{1,9},{9,17},{17,25},{25,1},{2,10},{10... | collective-permute-start | bytes 5480 | tf_op jit(solution)/shard_map/ppermute | solution.py:26
  79.7 1.8 %copy-start.2 = (f32[152,544]{1,0:T(8,128)S(1)}, f32[152,544]{1,0:T(8,128)}, u32[]{:S(2)}) copy-start(f32[152,544]{1,0:T(8,128)} %param.19) | copy-start | bytes 992260
  80.7 1.6 %copy-start.5 = (f32[3,544]{1,0:T(4,128)S(1)}, f32[3,544]{1,0:T(4,128)}, u32[]{:S(2)}) copy-start(f32[3,544]{1,0:T(4,128)} %param.16) | copy-start | bytes 19588
  92.1 49.7 %collective-permute-start.3 = (f32[1,3,152]{2,1,0:T(4,128)S(1)}, f32[1,3,152]{2,1,0:T(4,128)S(1)}, u32[]{:S(2)}, u32[]{:S(2)}) collective-permute-start(f32[1,3,152]{2,1,0:T(4,128)S(1)} %convolution_bitcast_fusion.2), channel_id=1, source_target_pairs={{0,8},{8,16},{16,24},{24,0},{1,9},{9,17},{17,25},{25,1},{2,10},{10... | collective-permute-start | bytes 5480 | tf_op jit(solution)/shard_map/ppermute | solution.py:26
  141.8 5.4 %collective-permute-start.4 = (f32[1,3,152]{2,1,0:T(4,128)S(1)}, f32[1,3,152]{2,1,0:T(4,128)S(1)}, u32[]{:S(2)}, u32[]{:S(2)}) collective-permute-start(f32[1,3,152]{2,1,0:T(4,128)S(1)} %collective-permute-done.3), channel_id=1, source_target_pairs={{0,8},{8,16},{16,24},{24,0},{1,9},{9,17},{17,25},{25,1},{2,10},{10... | collective-permute-start | bytes 5480 | tf_op jit(solution)/shard_map/ppermute | solution.py:26
  147.2 5.4 %collective-permute-start.5 = (f32[1,3,152]{2,1,0:T(4,128)S(1)}, f32[1,3,152]{2,1,0:T(4,128)S(1)}, u32[]{:S(2)}, u32[]{:S(2)}) collective-permute-start(f32[1,3,152]{2,1,0:T(4,128)S(1)} %collective-permute-done.4), channel_id=1, source_target_pairs={{0,8},{8,16},{16,24},{24,0},{1,9},{9,17},{17,25},{25,1},{2,10},{10... | collective-permute-start | bytes 5480 | tf_op jit(solution)/shard_map/ppermute | solution.py:26
